TPU v7x, 32 devices: a whole 2x2x4 slice. The times are simulated.
32 devices in a mesh: row: 4 (over y, core), col: 8 (over z, x).
Axes of the slice: x: 2, y: 2, z: 4, core: 2. Of those that a mesh axis runs over, the one named last changes fastest.
Arguments:
- object_field: float32 [2, 1024, 2048], P(None, 'row', 'col'), may hold values from -4 to 4
- modes: bfloat16 [4, 12, 2, 256, 256], P('row', None, None, 'col'), may hold values from -5 to 5
- coeffs: float32 [4, 8, 4, 12], P('row', 'col'), may hold values from -1.5 to 1.5
- offsets: int32 [4, 8, 4, 2], P('row', 'col'), may hold values from -128 to 128, as said below
- region: int32 [4, 8, 4], P('row', 'col'), may hold values from 0 to 3, as said below
- counts: int32 [4, 8], P('row', 'col'), may hold values from 1 to 4, as said below
- intensity: bfloat16 [4, 8, 4, 256, 256], P('row', 'col'), may hold values from 0.049804688 to 4
Outputs:
- object_grad: float32 [2, 1024, 2048], P(None, 'row', 'col')
- mode_grad: float32 [4, 12, 2, 256, 256], P('row', None, None, 'col')
Inputs may be any that keep to these rules, and one draw needn't show every extreme that they name: `offsets`: every window reaches at most 128 cells beyond its tile on each side; every tile has a live slot whose window starts at row offset -128 and column offset 256 - 256 / 2. A position's region is its tile's row index or the next one; slot 0 of every tile has its own row's region. Slots 0 to counts - 1 of a tile are live, the rest are ignored; some tile is full and some tile has one live slot.
All inputs are finite; a program needn't handle non-finite values.
Results may differ from a plain program's by a relative error of at most 0.014.
Values may be sent and summed in bfloat16 or wider, within the bound.
No kernel may reach another device: no remote copies, remote signals or barrier semaphores. Data moves between devices by JAX's collectives and lax.ppermute only.
A program may use at most 64 MiB of HBM per device.

v0:
```python
import math
import jax
import jax.numpy as jnp
from jax import lax
from jax.sharding import PartitionSpec as P

FLOOR = 0.25


def extended_2(x, sides, width):
    for axis, dim in sides:
        size, length = (lax.axis_size(axis), x.shape[dim])
        up = [(i, (i + 1) % size) for i in range(size - 1)]
        down = [(j, i) for i, j in up]
        last = lax.slice_in_dim(x, length - width, length, axis=dim)
        leading = lax.slice_in_dim(x, 0, width, axis=dim)
        before = lax.ppermute(last, axis, up)
        after = lax.ppermute(leading, axis, down)
        x = jnp.concatenate([before, x, after], axis=dim)
    return x


def from_behind(value, axis, steps):
    count = lax.axis_size(axis)
    leading, last = (max(0, -steps), min(count, count - steps))
    return lax.ppermute(value, axis, [(source, source + steps) for source in range(leading, last)])


def dft_tables(length):
    indices = jnp.arange(length, dtype=jnp.int32)
    phases = indices[:, None] * indices[None, :] % length
    angles = phases.astype(jnp.float32) * (2.0 * math.pi / length)
    scaling = 1.0 / math.sqrt(length)
    return (
        (jnp.cos(angles) * scaling).astype(jnp.bfloat16),
        (-jnp.sin(angles) * scaling).astype(jnp.bfloat16),
    )


def left_apply(table_re, table_im, real_part, imag_part, orient):

    def multiply(table, operand):
        return jnp.einsum("mr,prn->pmn", table, operand, preferred_element_type=jnp.float32)

    out_re = multiply(table_re, real_part) - orient * multiply(table_im, imag_part)
    out_im = multiply(table_re, imag_part) + orient * multiply(table_im, real_part)
    return (out_re, out_im)


def right_apply(table_re, table_im, real_part, imag_part, orient):

    def multiply(operand, table):
        return jnp.einsum("pmc,cn->pmn", operand, table, preferred_element_type=jnp.float32)

    out_re = multiply(real_part, table_re) - orient * multiply(imag_part, table_im)
    out_im = multiply(imag_part, table_re) + orient * multiply(real_part, table_im)
    return (out_re, out_im)


def local(object_field, modes, coeffs, offsets, region, counts, intensity):
    window_size = modes.shape[-1]
    half_size = window_size // 2
    num_modes = modes.shape[1]
    slot_count = coeffs.shape[2]
    row_index = lax.axis_index("row")
    object_low = object_field.astype(jnp.bfloat16)
    extended = extended_2(object_low, (("row", 1), ("col", 2)), half_size)
    follower = from_behind(modes, "row", -1)
    stacked = jnp.concatenate([modes[0], follower[0]], axis=0)
    stack_count = stacked.shape[0]
    weights = coeffs[0, 0]
    regions = region[0, 0]
    own_mask = (regions == row_index).astype(jnp.float32)
    next_mask = (regions == row_index + 1).astype(jnp.float32)
    mixing = jnp.concatenate([weights * own_mask[:, None], weights * next_mask[:, None]], axis=1)
    mixing_all = lax.all_gather(mixing, "col", axis=0, tiled=True)
    flattened = stacked.reshape(stack_count, -1).astype(jnp.float32)
    slabs = jnp.dot(
        mixing_all, flattened, precision=lax.Precision.HIGHEST, preferred_element_type=jnp.float32
    )
    slabs = slabs.reshape(mixing_all.shape[0], 2, stacked.shape[2], stacked.shape[3]).astype(
        jnp.bfloat16
    )
    probes = lax.all_to_all(slabs, "col", split_axis=0, concat_axis=2, tiled=True)
    corners = offsets[0, 0]

    def cut_window(corner):
        return lax.dynamic_slice(
            extended,
            (jnp.int32(0), corner[0] + half_size, corner[1] + half_size),
            (2, window_size, window_size),
        )

    windows = jax.vmap(cut_window)(corners)
    probe_re = probes[:, 0].astype(jnp.float32)
    probe_im = probes[:, 1].astype(jnp.float32)
    window_re = windows[:, 0].astype(jnp.float32)
    window_im = windows[:, 1].astype(jnp.float32)
    exit_re = (probe_re * window_re - probe_im * window_im).astype(jnp.bfloat16)
    exit_im = (probe_re * window_im + probe_im * window_re).astype(jnp.bfloat16)
    table_re, table_im = dft_tables(window_size)
    half_re, half_im = left_apply(table_re, table_im, exit_re, exit_im, 1.0)
    far_re, far_im = right_apply(
        table_re, table_im, half_re.astype(jnp.bfloat16), half_im.astype(jnp.bfloat16), 1.0
    )
    magnitude = jnp.sqrt(far_re * far_re + far_im * far_im)
    measured = jnp.sqrt(intensity[0, 0].astype(jnp.float32))
    live = (jnp.arange(slot_count, dtype=jnp.int32) < counts[0, 0]).astype(jnp.float32)
    factor = (measured / jnp.maximum(magnitude, FLOOR) - 1.0) * live[:, None, None]
    change_re = (far_re * factor).astype(jnp.bfloat16)
    change_im = (far_im * factor).astype(jnp.bfloat16)
    back_re, back_im = left_apply(table_re, table_im, change_re, change_im, -1.0)
    update_re, update_im = right_apply(
        table_re, table_im, back_re.astype(jnp.bfloat16), back_im.astype(jnp.bfloat16), -1.0
    )
    object_terms = jnp.stack(
        [probe_re * update_re + probe_im * update_im, probe_re * update_im - probe_im * update_re],
        axis=1,
    )
    terms = jnp.stack(
        [
            window_re * update_re + window_im * update_im,
            window_re * update_im - window_im * update_re,
        ],
        axis=1,
    ).astype(jnp.bfloat16)

    def place(position, accum):
        start_row = corners[position, 0] + half_size
        start_col = corners[position, 1] + half_size
        current = lax.dynamic_slice(
            accum, (jnp.int32(0), start_row, start_col), (2, window_size, window_size)
        )
        return lax.dynamic_update_slice(
            accum, current + object_terms[position], (jnp.int32(0), start_row, start_col)
        )

    accum = lax.fori_loop(0, slot_count, place, jnp.zeros(extended.shape, jnp.float32))
    received = lax.all_to_all(terms, "col", split_axis=2, concat_axis=0, tiled=True)
    col_count = lax.axis_size("col")
    per_source = jnp.einsum(
        "dpk,dpx->dkx",
        mixing_all.reshape(col_count, slot_count, -1),
        received.reshape(col_count, slot_count, -1).astype(jnp.float32),
        precision=lax.Precision.HIGHEST,
        preferred_element_type=jnp.float32,
    )
    rounded = lax.optimization_barrier(per_source.astype(jnp.bfloat16)).astype(jnp.float32)
    summed = jnp.sum(rounded, axis=0).reshape(stack_count, 2, received.shape[2], window_size)
    own_sum = summed[:num_modes]
    passed = from_behind(summed[num_modes:].astype(jnp.bfloat16), "row", 1).astype(jnp.float32)
    mode_grad = (own_sum + passed)[None]
    outer_rows = jnp.concatenate([accum[:, :half_size], accum[:, -half_size:]], axis=1)
    got_rows = extended_2(outer_rows.astype(jnp.bfloat16), (("row", 1),), half_size).astype(
        outer_rows.dtype
    )
    middle = accum[:, half_size:-half_size]
    middle = middle.at[:, :half_size].add(got_rows[:, :half_size])
    middle = middle.at[:, -half_size:].add(got_rows[:, -half_size:])
    outer_cols = jnp.concatenate([middle[:, :, :half_size], middle[:, :, -half_size:]], axis=2)
    got_cols = extended_2(outer_cols.astype(jnp.bfloat16), (("col", 2),), half_size).astype(
        outer_cols.dtype
    )
    object_grad = middle[:, :, half_size:-half_size]
    object_grad = object_grad.at[:, :, :half_size].add(got_cols[:, :, :half_size])
    object_grad = object_grad.at[:, :, -half_size:].add(got_cols[:, :, -half_size:])
    return (object_grad, mode_grad)


def solution(mesh):
    in_specs = (
        P(None, "row", "col"),
        P("row", None, None, "col", None),
        P("row", "col", None, None),
        P("row", "col", None, None),
        P("row", "col", None),
        P("row", "col"),
        P("row", "col", None, None, None),
    )
    out_specs = (P(None, "row", "col"), P("row", None, None, "col", None))
    return jax.shard_map(local, mesh=mesh, in_specs=in_specs, out_specs=out_specs, check_vma=False)
```

profile of v0, /device:TPU:30, one launch (start us, length us, event | category | flops | bytes accessed | tf_op | source)
XLA Modules:
  0.0 194.7 jit_solution(16721502046755920107)
XLA Ops:
  1.7 1.9 collective-permute-start.1
  3.7 3.6 %collective-permute-start.2 = (bf16[2,128,256]{2,1,0:T(8,128)(2,1)S(1)}, bf16[2,128,256]{2,1,0:T(8,128)(2,1)S(1)}, u32[]{:S(2)}, u32[]{:S(2)}) collective-permute-start(bf16[2,128,256]{2,1,0:T(8,128)(2,1)S(1)} %get-tuple-element.244), channel_id=1, source_target_pairs={{8,0},{16,8},{24,16},{9,1},{17,9},{25,17},{10,2},{18,10},{26,18},{... | collective-permute-start | bytes 393224 | tf_op jit(solution)/shard_map/ppermute | solution.py:18
  7.3 1.9 collective-permute-start
  10.7 1.3 concatenate.41
  12.0 24.6 %all-gather = f32[8,4,24]{2,1,0:T(4,128)S(1)} all-gather(f32[1,4,24]{2,1,0:T(4,128)S(1)} %maximum_bitcast_fusion), channel_id=1, replica_groups=mesh['row'=4,'col'=8] {'col'}, dimensions={0}, use_global_device_ids=true | all-gather | bytes 3456 | tf_op jit(solution)/shard_map/all_gather | solution.py:76
  36.8 1.3 collective-permute-start.3
  38.1 5.3 %collective-permute-start.4 = (bf16[2,512,128]{2,1,0:T(8,128)(2,1)S(1)}, bf16[2,512,128]{2,1,0:T(8,128)(2,1)}, u32[]{:S(2)}, u32[]{:S(2)}) collective-permute-start(bf16[2,512,128]{2,1,0:T(8,128)(2,1)S(1)} %get-tuple-element.242), channel_id=1, source_target_pairs={{1,0},{2,1},{3,2},{4,3},{5,4},{6,5},{7,6},{9,8},{10,9},{11,10},{12... | collective-permute-start | bytes 786440 | tf_op jit(solution)/shard_map/ppermute | solution.py:18
  45.3 1.6 copy.58
  46.8 6.0 %all-to-all-start = ((bf16[32,2,32,256]{3,2,1,0:T(8,128)(2,1)}), bf16[32,2,32,256]{3,2,1,0:T(8,128)(2,1)S(1)}, u32[]{:S(2)}, u32[]{:S(2)}) async-start(bf16[32,2,32,256]{3,2,1,0:T(8,128)(2,1)} %copy.58), calls=%async_computation | async-start | bytes 2097152 | tf_op jit(solution)/shard_map/all_to_all | solution.py:84
  56.7 11.2 %while.22 = (s32[]{:T(128)}, bf16[2,512,512]{2,1,0:T(8,128)(2,1)S(1)}, s32[4,3]{1,0:T(4,128)}, bf16[4,2,256,256]{3,2,0,1:T(8,128)(2,1)S(1)}, s32[]{:T(128)}) while((s32[]{:T(128)}, bf16[2,512,512]{2,1,0:T(8,128)(2,1)S(1)}, s32[4,3]{1,0:T(4,128)}, bf16[4,2,256,256]{3,2,0,1:T(8,128)(2,1)S(1)}, s32[]{:T(128)}) %tuple.95), condition=%wide.while_cond.4, body=%wide.while_body.4.sunk | while | flops 2 | bytes 524413 | solution.py:88
  58.0 1.5 bitcast_dynamic-update-slice_fusion.2
  60.7 1.5 bitcast_dynamic-update-slice_fusion.2
  63.5 1.5 bitcast_dynamic-update-slice_fusion.2
  66.3 1.5 bitcast_dynamic-update-slice_fusion.2
  67.9 4.4 %all-to-all-done = bf16[32,2,32,256]{3,2,1,0:T(8,128)(2,1)S(1)} async-done(((bf16[32,2,32,256]{3,2,1,0:T(8,128)(2,1)}), bf16[32,2,32,256]{3,2,1,0:T(8,128)(2,1)S(1)}, u32[]{:S(2)}, u32[]{:S(2)}) %all-to-all-start) | async-done | bytes 1048608 | tf_op jit(solution)/shard_map/all_to_all | solution.py:84
  75.4 1.3 fusion.9
  76.6 1.3 fusion.8
  77.9 1.3 fusion.57
  80.4 1.3 convolution_add_fusion
  81.7 2.0 %multiply_convert_fusion.1 = (bf16[4,256,256]{2,1,0:T(8,128)(2,1)S(1)}, bf16[4,256,256]{2,1,0:T(8,128)(2,1)S(1)}) fusion(f32[4]{0:T(128)S(1)} %copy-done.7, f32[4,256,256]{2,1,0:T(8,128)S(1)} %convolution_add_fusion, bf16[1,1,4,256,256]{4,3,2,1,0:T(8,128)(2,1)S(1)} %copy-done.6, f32[4,256,256]{2,1,0:T(8,128)S(1)} %fusion.61, bf16[4,256,256]{1,2,0:T(8,128)(2,1)S(1)} %fusion.8), kind=kOutput, calls=%fused_computation.61 | convolution fusion | flops 138739712 | bytes 4194320 | tf_op jit(solution)/shard_map/pmc,cn->pmn/dot_general | solution.py:53
  83.7 1.5 fusion.55
  86.5 1.3 fusion.11
  87.7 1.3 fusion.10
  90.2 1.3 fusion.53
  91.5 1.3 fusion
  92.8 1.8 fusion.28
  94.7 1.8 copy.80
  96.5 6.7 %all-to-all-start.1 = ((bf16[4,2,256,256]{3,0,1,2:T(4,128)(2,1)}), bf16[4,2,256,256]{3,0,1,2:T(4,128)(2,1)}, u32[]{:S(2)}, u32[]{:S(2)}) async-start(bf16[4,2,256,256]{3,0,1,2:T(4,128)(2,1)} %copy.80), calls=%async_computation.1 | async-start | bytes 2097152 | tf_op jit(solution)/shard_map/all_to_all | solution.py:139
  103.2 1.6 pad_maximum_fusion
  105.5 53.2 %while.21 = (s32[]{:T(128)}, f32[2,512,512]{2,1,0:T(8,128)S(1)}, s32[4,2]{0,1:T(2,128)S(1)}, f32[4,2,256,256]{3,2,0,1:T(8,128)}, s32[]{:T(128)}, /*index=5*/s32[1,1]{0,1:T(1,128)}, s32[]{:T(128)}, s32[1,1]{0,1:T(1,128)}) while((s32[]{:T(128)}, f32[2,512,512]{2,1,0:T(8,128)S(1)}, s32[4,2]{0,1:T(2,128)S(1)}, f32[4,2,256,256]{3,2,0,1:T(8,128)}, ...), condition=%wide.region_1.2_spmd, body=%wide.region_0.1_spmd.sunk | while | flops 131082 | bytes 2621661 | solution.py:138
  108.7 1.3 bitcast_add_fusion.2
  109.9 6.0 %dynamic_update_slice.12 = f32[2,512,512]{2,1,0:T(8,128)S(1)} dynamic-update-slice(f32[2,512,512]{2,1,0:T(8,128)S(1)} %get-tuple-element.333, f32[2,256,256]{2,1,0:T(8,128)S(1)} %bitcast_add_fusion.2, s32[]{:T(128)} %constant.199.clone.1..sunk, s32[]{:T(128)S(6)} %select_n.116, s32[]{:T(128)S(6)} %select_n.117) | dynamic-update-slice | bytes 1048580 | tf_op jit(solution)/shard_map/while/body/eval_jaxpr/dynamic_update_slice | solution.py:134
  119.1 1.3 bitcast_add_fusion.2
  120.4 8.7 %dynamic_update_slice.12 = f32[2,512,512]{2,1,0:T(8,128)S(1)} dynamic-update-slice(f32[2,512,512]{2,1,0:T(8,128)S(1)} %get-tuple-element.333, f32[2,256,256]{2,1,0:T(8,128)S(1)} %bitcast_add_fusion.2, s32[]{:T(128)} %constant.199.clone.1..sunk, s32[]{:T(128)S(6)} %select_n.116, s32[]{:T(128)S(6)} %select_n.117) | dynamic-update-slice | bytes 1048580 | tf_op jit(solution)/shard_map/while/body/eval_jaxpr/dynamic_update_slice | solution.py:134
  132.3 1.3 bitcast_add_fusion.2
  133.6 10.2 %dynamic_update_slice.12 = f32[2,512,512]{2,1,0:T(8,128)S(1)} dynamic-update-slice(f32[2,512,512]{2,1,0:T(8,128)S(1)} %get-tuple-element.333, f32[2,256,256]{2,1,0:T(8,128)S(1)} %bitcast_add_fusion.2, s32[]{:T(128)} %constant.199.clone.1..sunk, s32[]{:T(128)S(6)} %select_n.116, s32[]{:T(128)S(6)} %select_n.117) | dynamic-update-slice | bytes 1048580 | tf_op jit(solution)/shard_map/while/body/eval_jaxpr/dynamic_update_slice | solution.py:134
  147.0 1.3 bitcast_add_fusion.2
  148.3 10.4 %dynamic_update_slice.12 = f32[2,512,512]{2,1,0:T(8,128)S(1)} dynamic-update-slice(f32[2,512,512]{2,1,0:T(8,128)S(1)} %get-tuple-element.333, f32[2,256,256]{2,1,0:T(8,128)S(1)} %bitcast_add_fusion.2, s32[]{:T(128)} %constant.199.clone.1..sunk, s32[]{:T(128)S(6)} %select_n.116, s32[]{:T(128)S(6)} %select_n.117) | dynamic-update-slice | bytes 1048580 | tf_op jit(solution)/shard_map/while/body/eval_jaxpr/dynamic_update_slice | solution.py:134
  158.9 2.2 %collective-permute-start.5 = (bf16[2,128,512]{2,1,0:T(8,128)(2,1)S(1)}, bf16[2,128,512]{2,1,0:T(8,128)(2,1)S(1)}, u32[]{:S(2)}, u32[]{:S(2)}) collective-permute-start(bf16[2,128,512]{2,1,0:T(8,128)(2,1)S(1)} %get-tuple-element.237), channel_id=1, source_target_pairs={{0,8},{8,16},{16,24},{1,9},{9,17},{17,25},{2,10},{10,18},{18,26},{... | collective-permute-start | bytes 786440 | tf_op jit(solution)/shard_map/ppermute | solution.py:17
  161.1 3.6 %collective-permute-start.6 = (bf16[2,128,512]{2,1,0:T(8,128)(2,1)S(1)}, bf16[2,128,512]{2,1,0:T(8,128)(2,1)S(1)}, u32[]{:S(2)}, u32[]{:S(2)}) collective-permute-start(bf16[2,128,512]{2,1,0:T(8,128)(2,1)S(1)} %get-tuple-element.238), channel_id=1, source_target_pairs={{8,0},{16,8},{24,16},{9,1},{17,9},{25,17},{10,2},{18,10},{26,18},{... | collective-permute-start | bytes 786440 | tf_op jit(solution)/shard_map/ppermute | solution.py:18
  164.8 1.8 collective-permute-done.5
  166.6 2.0 %collective-permute-done.6 = bf16[2,128,512]{2,1,0:T(8,128)(2,1)S(1)} collective-permute-done((bf16[2,128,512]{2,1,0:T(8,128)(2,1)S(1)}, bf16[2,128,512]{2,1,0:T(8,128)(2,1)S(1)}, u32[]{:S(2)}, u32[]{:S(2)}) %collective-permute-start.6) | collective-permute-done | bytes 262176 | tf_op jit(solution)/shard_map/ppermute | solution.py:18
  169.9 1.3 collective-permute-start.7
  171.2 4.6 %collective-permute-start.8 = (bf16[2,256,128]{2,1,0:T(8,128)(2,1)S(1)}, bf16[2,256,128]{2,1,0:T(8,128)(2,1)S(1)}, u32[]{:S(2)}, u32[]{:S(2)}) collective-permute-start(bf16[2,256,128]{2,1,0:T(8,128)(2,1)S(1)} %get-tuple-element.240), channel_id=1, source_target_pairs={{1,0},{2,1},{3,2},{4,3},{5,4},{6,5},{7,6},{9,8},{10,9},{11,10},{12... | collective-permute-start | bytes 393224 | tf_op jit(solution)/shard_map/ppermute | solution.py:18
  175.7 1.5 copy.109
  178.0 5.5 %convolution_convert_fusion = bf16[8,24,16384]{2,1,0:T(8,128)(2,1)S(1)} fusion(f32[8,4,24]{2,1,0:T(4,128)S(1)} %all-gather, bf16[8,4,16384]{2,1,0:T(4,128)(2,1)S(1)} %reshape.183), kind=kOutput, calls=%fused_computation.5 | convolution fusion | flops 154140672 | bytes 7343104 | tf_op jit(solution)/shard_map/dpk,dpx->dkx/dot_general | solution.py:141
  184.6 1.9 collective-permute-start.9
  188.5 5.3 %collective-permute-done.9 = bf16[12,2,32,256]{3,2,1,0:T(8,128)(2,1)S(1)} collective-permute-done((bf16[12,2,32,256]{3,2,1,0:T(8,128)(2,1)S(1)}, bf16[12,2,32,256]{3,2,1,0:T(8,128)(2,1)S(1)}, u32[]{:S(2)}, u32[]{:S(2)}) %collective-permute-start.9) | collective-permute-done | bytes 393248 | tf_op jit(solution)/shard_map/ppermute | solution.py:26
  (82 shorter events, 29.0 us)
Async XLA Ops:
  1.7 34.9 %collective-permute-start.1 = (bf16[2,128,256]{2,1,0:T(8,128)(2,1)S(1)}, bf16[2,128,256]{2,1,0:T(8,128)(2,1)S(1)}, u32[]{:S(2)}, u32[]{:S(2)}) collective-permute-start(bf16[2,128,256]{2,1,0:T(8,128)(2,1)S(1)} %get-tuple-element.243), channel_id=1, source_target_pairs={{0,8},{8,16},{16,24},{1,9},{9,17},{17,25},{2,10},{10,18},{18,26},{... | collective-permute-start | bytes 393224 | tf_op jit(solution)/shard_map/ppermute | solution.py:17
  3.7 33.0 %collective-permute-start.2 = (bf16[2,128,256]{2,1,0:T(8,128)(2,1)S(1)}, bf16[2,128,256]{2,1,0:T(8,128)(2,1)S(1)}, u32[]{:S(2)}, u32[]{:S(2)}) collective-permute-start(bf16[2,128,256]{2,1,0:T(8,128)(2,1)S(1)} %get-tuple-element.244), channel_id=1, source_target_pairs={{8,0},{16,8},{24,16},{9,1},{17,9},{25,17},{10,2},{18,10},{26,18},{... | collective-permute-start | bytes 393224 | tf_op jit(solution)/shard_map/ppermute | solution.py:18
  7.3 36.0 %collective-permute-start = (bf16[1,12,2,32,256]{4,3,2,1,0:T(8,128)(2,1)}, bf16[1,12,2,32,256]{4,3,2,1,0:T(8,128)(2,1)S(1)}, u32[]{:S(2)}, u32[]{:S(2)}) collective-permute-start(bf16[1,12,2,32,256]{4,3,2,1,0:T(8,128)(2,1)} %param.18), channel_id=1, source_target_pairs={{8,0},{16,8},{24,16},{9,1},{17,9},{25,17},{10,2},{18,10},{26,18},{... | collective-permute-start | bytes 1179656 | tf_op jit(solution)/shard_map/ppermute | solution.py:26
  36.6 7.2 %copy-start.2 = (bf16[2,128,256]{2,1,0:T(8,128)(2,1)}, bf16[2,128,256]{2,1,0:T(8,128)(2,1)S(1)}, u32[]{:S(2)}) copy-start(bf16[2,128,256]{2,1,0:T(8,128)(2,1)S(1)} %collective-permute-done.2) | copy-start | bytes 393220
  36.8 18.0 %collective-permute-start.3 = (bf16[2,512,128]{2,1,0:T(8,128)(2,1)S(1)}, bf16[2,512,128]{2,1,0:T(8,128)(2,1)S(1)}, u32[]{:S(2)}, u32[]{:S(2)}) collective-permute-start(bf16[2,512,128]{2,1,0:T(8,128)(2,1)S(1)} %get-tuple-element.241), channel_id=1, source_target_pairs={{0,1},{1,2},{2,3},{3,4},{4,5},{5,6},{6,7},{8,9},{9,10},{10,11},{11... | collective-permute-start | bytes 786440 | tf_op jit(solution)/shard_map/ppermute | solution.py:17
  38.1 17.4 %collective-permute-start.4 = (bf16[2,512,128]{2,1,0:T(8,128)(2,1)S(1)}, bf16[2,512,128]{2,1,0:T(8,128)(2,1)}, u32[]{:S(2)}, u32[]{:S(2)}) collective-permute-start(bf16[2,512,128]{2,1,0:T(8,128)(2,1)S(1)} %get-tuple-element.242), channel_id=1, source_target_pairs={{1,0},{2,1},{3,2},{4,3},{5,4},{6,5},{7,6},{9,8},{10,9},{11,10},{12... | collective-permute-start | bytes 786440 | tf_op jit(solution)/shard_map/ppermute | solution.py:18
  45.3 7.6 %copy-start.4 = (s32[1,1,4,2]{2,3,1,0:T(2,128)S(1)}, s32[1,1,4,2]{2,3,1,0:T(2,128)}, u32[]{:S(2)}) copy-start(s32[1,1,4,2]{2,3,1,0:T(2,128)} %param.20) | copy-start | bytes 100
  46.8 25.5 %all-to-all-start = ((bf16[32,2,32,256]{3,2,1,0:T(8,128)(2,1)}), bf16[32,2,32,256]{3,2,1,0:T(8,128)(2,1)S(1)}, u32[]{:S(2)}, u32[]{:S(2)}) async-start(bf16[32,2,32,256]{3,2,1,0:T(8,128)(2,1)} %copy.58), calls=%async_computation | async-start | bytes 2097152 | tf_op jit(solution)/shard_map/all_to_all | solution.py:84
  54.8 0.7 copy-start.3
  79.1 2.5 %copy-start.6 = (bf16[1,1,4,256,256]{4,3,2,1,0:T(8,128)(2,1)S(1)}, bf16[1,1,4,256,256]{4,3,2,1,0:T(8,128)(2,1)}, u32[]{:S(2)}) copy-start(bf16[1,1,4,256,256]{4,3,2,1,0:T(8,128)(2,1)} %param.23) | copy-start | bytes 1572868
  79.1 2.5 %copy-start.7 = (f32[4]{0:T(128)S(1)}, f32[4]{0:T(128)}, u32[]{:S(2)}) copy-start(f32[4]{0:T(128)} %compare_convert_fusion) | copy-start | bytes 52
  96.5 79.3 %all-to-all-start.1 = ((bf16[4,2,256,256]{3,0,1,2:T(4,128)(2,1)}), bf16[4,2,256,256]{3,0,1,2:T(4,128)(2,1)}, u32[]{:S(2)}, u32[]{:S(2)}) async-start(bf16[4,2,256,256]{3,0,1,2:T(4,128)(2,1)} %copy.80), calls=%async_computation.1 | async-start | bytes 2097152 | tf_op jit(solution)/shard_map/all_to_all | solution.py:139
  104.8 0.7 copy-start.5
  158.9 7.7 %collective-permute-start.5 = (bf16[2,128,512]{2,1,0:T(8,128)(2,1)S(1)}, bf16[2,128,512]{2,1,0:T(8,128)(2,1)S(1)}, u32[]{:S(2)}, u32[]{:S(2)}) collective-permute-start(bf16[2,128,512]{2,1,0:T(8,128)(2,1)S(1)} %get-tuple-element.237), channel_id=1, source_target_pairs={{0,8},{8,16},{16,24},{1,9},{9,17},{17,25},{2,10},{10,18},{18,26},{... | collective-permute-start | bytes 786440 | tf_op jit(solution)/shard_map/ppermute | solution.py:17
  161.1 7.5 %collective-permute-start.6 = (bf16[2,128,512]{2,1,0:T(8,128)(2,1)S(1)}, bf16[2,128,512]{2,1,0:T(8,128)(2,1)S(1)}, u32[]{:S(2)}, u32[]{:S(2)}) collective-permute-start(bf16[2,128,512]{2,1,0:T(8,128)(2,1)S(1)} %get-tuple-element.238), channel_id=1, source_target_pairs={{8,0},{16,8},{24,16},{9,1},{17,9},{25,17},{10,2},{18,10},{26,18},{... | collective-permute-start | bytes 786440 | tf_op jit(solution)/shard_map/ppermute | solution.py:18
  168.8 1.0 copy-start
  169.9 16.7 %collective-permute-start.7 = (bf16[2,256,128]{2,1,0:T(8,128)(2,1)S(1)}, bf16[2,256,128]{2,1,0:T(8,128)(2,1)S(1)}, u32[]{:S(2)}, u32[]{:S(2)}) collective-permute-start(bf16[2,256,128]{2,1,0:T(8,128)(2,1)S(1)} %get-tuple-element.239), channel_id=1, source_target_pairs={{0,1},{1,2},{2,3},{3,4},{4,5},{5,6},{6,7},{8,9},{9,10},{10,11},{11... | collective-permute-start | bytes 393224 | tf_op jit(solution)/shard_map/ppermute | solution.py:17
  171.2 15.4 %collective-permute-start.8 = (bf16[2,256,128]{2,1,0:T(8,128)(2,1)S(1)}, bf16[2,256,128]{2,1,0:T(8,128)(2,1)S(1)}, u32[]{:S(2)}, u32[]{:S(2)}) collective-permute-start(bf16[2,256,128]{2,1,0:T(8,128)(2,1)S(1)} %get-tuple-element.240), channel_id=1, source_target_pairs={{1,0},{2,1},{3,2},{4,3},{5,4},{6,5},{7,6},{9,8},{10,9},{11,10},{12... | collective-permute-start | bytes 393224 | tf_op jit(solution)/shard_map/ppermute | solution.py:18
  184.6 9.1 %collective-permute-start.9 = (bf16[12,2,32,256]{3,2,1,0:T(8,128)(2,1)S(1)}, bf16[12,2,32,256]{3,2,1,0:T(8,128)(2,1)S(1)}, u32[]{:S(2)}, u32[]{:S(2)}) collective-permute-start(bf16[12,2,32,256]{3,2,1,0:T(8,128)(2,1)S(1)} %bitcast.189), channel_id=1, source_target_pairs={{0,8},{8,16},{16,24},{1,9},{9,17},{17,25},{2,10},{10,18},{18,26},{... | collective-permute-start | bytes 1179656 | tf_op jit(solution)/shard_map/ppermute | solution.py:26
  187.6 0.8 copy-start.1
where the time goes:
time: 196 us; the launch traced here: 195 us
  local copies, waits for them, and re-layouts  60.4 us (31%)
  starting transfers between devices  40.3 us (21%)
  matrix products  28.3 us (14%)
  blocking collectives  24.6 us (13%)
  other arithmetic  15 us (8%)
  waiting for transfers between devices  13.5 us (7%)
  loops' own time  10.8 us (6%)
    dynamic_update_slice x4, local copies, waits for them, and re-layouts, place(): lax.dynamic_update_slice(accum, current + object_terms[position], (jnp.in...  35.3 us
    all_gather x1, blocking collectives, local(): mixing_all = lax.all_gather(mixing, 'col', axis=0, tiled=True)  24.6 us
    ppermute x4, starting transfers between devices, extended_2(): after = lax.ppermute(leading, axis, down)  17.1 us
    dot_general x8, matrix products, multiply(): jnp.einsum('pmc,cn->pmn', operand, table, preferred_element_type=jnp.floa...  11.4 us
    gather x12, local copies, waits for them, and re-layouts  11 us
    another operation x1, loops' own time, local(): lax.fori_loop(0, slot_count, place, jnp.zeros(extended.shape, jnp.float32))  10.5 us
    dot_general x8, matrix products, multiply(): jnp.einsum('mr,prn->pmn', table, operand, preferred_element_type=jnp.floa...  10.2 us
    all_to_all x1, starting transfers between devices, local(): lax.all_to_all(terms, 'col', split_axis=2, concat_axis=0, tiled=True)  6.72 us
  transfers between devices with their start and end apart: 12, of which 4 were waited for; matrix products, arithmetic and copies ran while one was open for 39% of the time, Pallas kernels for 0%

commit v1 on v0

--- a/solution.py
+++ b/solution.py
@@ -73,7 +73,14 @@
     own_mask = (regions == row_index).astype(jnp.float32)
     next_mask = (regions == row_index + 1).astype(jnp.float32)
     mixing = jnp.concatenate([weights * own_mask[:, None], weights * next_mask[:, None]], axis=1)
-    mixing_all = lax.all_gather(mixing, "col", axis=0, tiled=True)
+    n_dev = lax.axis_size("col")
+    right = [(i_2, (i_2 + 1) % n_dev) for i_2 in range(n_dev)]
+    blocks = [mixing]
+    for reach in range(1, n_dev):
+        blocks = [lax.ppermute(blocks[0], "col", right), *blocks]
+    whole = jnp.concatenate(blocks, axis=0)
+    shift = (lax.axis_index("col") + 1) * blocks[-1].shape[0]
+    mixing_all = jnp.roll(whole, shift, axis=0)
     flattened = stacked.reshape(stack_count, -1).astype(jnp.float32)
     slabs = jnp.dot(
         mixing_all, flattened, precision=lax.Precision.HIGHEST, preferred_element_type=jnp.float32

time: 196 us -> 205 us (1.046)
  starting transfers between devices: 40.3 us -> 67.8 us
  blocking collectives: 24.6 us -> 0 us
  waiting for transfers between devices: 13.5 us -> 20 us
    ppermute x0 -> x7, starting transfers between devices: none -> 27.5 us  [local(): blocks = [lax.ppermute(blocks[0], 'col', right), *blocks]]
    all_gather x1 -> x0, blocking collectives: 24.6 us -> none  [local(): mixing_all = lax.all_gather(mixing, 'col', axis=0, tiled=True)]
    ppermute x0 -> x7, waiting for transfers between devices: none -> 9.26 us  [local(): blocks = [lax.ppermute(blocks[0], 'col', right), *blocks]]
    all_to_all x1, waiting for transfers between devices: 4.41 us -> 1.71 us  [local(): lax.all_to_all(slabs, 'col', split_axis=0, concat_axis=2, tiled=True)]
  transfers between devices with their start and end apart: 12 -> 19, of which waited for: 4 -> 10; matrix products, arithmetic and copies ran while one was open for 39% -> 37% of each run, Pallas kernels for 0% -> 0%
where the time goes in v1:
time: 205 us; the launch traced here: 203 us
  starting transfers between devices  67.8 us (33%)
  local copies, waits for them, and re-layouts  59.8 us (29%)
  matrix products  28.3 us (14%)
  waiting for transfers between devices  20 us (10%)
  other arithmetic  14.9 us (7%)
  loops' own time  10.8 us (5%)
    dynamic_update_slice x4, local copies, waits for them, and re-layouts, place(): lax.dynamic_update_slice(accum, current + object_terms[position], (jnp.in...  35.3 us
    ppermute x7, starting transfers between devices, local(): blocks = [lax.ppermute(blocks[0], 'col', right), *blocks]  27.5 us
    ppermute x4, starting transfers between devices, extended_2(): after = lax.ppermute(leading, axis, down)  17.1 us
    dot_general x8, matrix products, multiply(): jnp.einsum('pmc,cn->pmn', operand, table, preferred_element_type=jnp.floa...  11.4 us
    gather x12, local copies, waits for them, and re-layouts  11.2 us
    another operation x1, loops' own time, local(): lax.fori_loop(0, slot_count, place, jnp.zeros(extended.shape, jnp.float32))  10.5 us
    dot_general x8, matrix products, multiply(): jnp.einsum('mr,prn->pmn', table, operand, preferred_element_type=jnp.floa...  10.2 us
    ppermute x7, waiting for transfers between devices, local(): blocks = [lax.ppermute(blocks[0], 'col', right), *blocks]  9.26 us
  transfers between devices with their start and end apart: 19, of which 10 were waited for; matrix products, arithmetic and copies ran while one was open for 37% of the time, Pallas kernels for 0%

profile of v1, /device:TPU:30, one launch (start us, length us, event | category | flops | bytes accessed | tf_op | source)
XLA Modules:
  0.0 203.5 jit_solution(8888020733432683714)
XLA Ops:
  1.7 1.9 collective-permute-start.8
  3.7 3.6 %collective-permute-start.9 = (bf16[2,128,256]{2,1,0:T(8,128)(2,1)S(1)}, bf16[2,128,256]{2,1,0:T(8,128)(2,1)S(1)}, u32[]{:S(2)}, u32[]{:S(2)}) collective-permute-start(bf16[2,128,256]{2,1,0:T(8,128)(2,1)S(1)} %get-tuple-element.244), channel_id=1, source_target_pairs={{8,0},{16,8},{24,16},{9,1},{17,9},{25,17},{10,2},{18,10},{26,18},{... | collective-permute-start | bytes 393224 | tf_op jit(solution)/shard_map/ppermute | solution.py:18
  9.1 3.5 %collective-permute-done = f32[4,24]{0,1:T(8,128)S(1)} collective-permute-done((f32[4,24]{0,1:T(8,128)S(1)}, f32[4,24]{0,1:T(8,128)S(1)}, u32[]{:S(2)}, u32[]{:S(2)}) %collective-permute-start) | collective-permute-done | bytes 416 | tf_op jit(solution)/shard_map/ppermute | solution.py:80
  12.6 2.9 %collective-permute-start.1 = (f32[4,24]{0,1:T(8,128)S(1)}, f32[4,24]{0,1:T(8,128)S(1)}, u32[]{:S(2)}, u32[]{:S(2)}) collective-permute-start(f32[4,24]{0,1:T(8,128)S(1)} %collective-permute-done), channel_id=1, source_target_pairs={{0,1},{1,2},{2,3},{3,4},{4,5},{5,6},{6,7},{7,0},{8,9},{9,10},{10,1... | collective-permute-start | bytes 1160 | tf_op jit(solution)/shard_map/ppermute | solution.py:80
  15.5 1.4 collective-permute-done.1
  16.9 5.0 %collective-permute-start.2 = (f32[4,24]{0,1:T(8,128)S(1)}, f32[4,24]{0,1:T(8,128)S(1)}, u32[]{:S(2)}, u32[]{:S(2)}) collective-permute-start(f32[4,24]{0,1:T(8,128)S(1)} %collective-permute-done.1), channel_id=1, source_target_pairs={{0,1},{1,2},{2,3},{3,4},{4,5},{5,6},{6,7},{7,0},{8,9},{9,10},{10,1... | collective-permute-start | bytes 1160 | tf_op jit(solution)/shard_map/ppermute | solution.py:80
  21.9 1.4 collective-permute-done.2
  23.3 5.0 %collective-permute-start.3 = (f32[4,24]{0,1:T(8,128)S(1)}, f32[4,24]{0,1:T(8,128)S(1)}, u32[]{:S(2)}, u32[]{:S(2)}) collective-permute-start(f32[4,24]{0,1:T(8,128)S(1)} %collective-permute-done.2), channel_id=1, source_target_pairs={{0,1},{1,2},{2,3},{3,4},{4,5},{5,6},{6,7},{7,0},{8,9},{9,10},{10,1... | collective-permute-start | bytes 1160 | tf_op jit(solution)/shard_map/ppermute | solution.py:80
  28.3 1.9 collective-permute-start.7
  30.2 4.5 %collective-permute-start.4 = (f32[4,24]{0,1:T(8,128)S(1)}, f32[4,24]{0,1:T(8,128)S(1)}, u32[]{:S(2)}, u32[]{:S(2)}) collective-permute-start(f32[4,24]{0,1:T(8,128)S(1)} %collective-permute-done.3), channel_id=1, source_target_pairs={{0,1},{1,2},{2,3},{3,4},{4,5},{5,6},{6,7},{7,0},{8,9},{9,10},{10,1... | collective-permute-start | bytes 1160 | tf_op jit(solution)/shard_map/ppermute | solution.py:80
  34.7 1.4 collective-permute-done.4
  36.1 5.0 %collective-permute-start.5 = (f32[4,24]{0,1:T(8,128)S(1)}, f32[4,24]{0,1:T(8,128)S(1)}, u32[]{:S(2)}, u32[]{:S(2)}) collective-permute-start(f32[4,24]{0,1:T(8,128)S(1)} %collective-permute-done.4), channel_id=1, source_target_pairs={{0,1},{1,2},{2,3},{3,4},{4,5},{5,6},{6,7},{7,0},{8,9},{9,10},{10,1... | collective-permute-start | bytes 1160 | tf_op jit(solution)/shard_map/ppermute | solution.py:80
  41.1 1.3 concatenate.48
  42.5 5.0 %collective-permute-start.6 = (f32[4,24]{0,1:T(8,128)S(1)}, f32[4,24]{0,1:T(8,128)S(1)}, u32[]{:S(2)}, u32[]{:S(2)}) collective-permute-start(f32[4,24]{0,1:T(8,128)S(1)} %collective-permute-done.5), channel_id=1, source_target_pairs={{0,1},{1,2},{2,3},{3,4},{4,5},{5,6},{6,7},{7,0},{8,9},{9,10},{10,1... | collective-permute-start | bytes 1160 | tf_op jit(solution)/shard_map/ppermute | solution.py:80
  47.4 1.4 collective-permute-done.6
  49.2 1.3 collective-permute-start.10
  50.5 5.2 %collective-permute-start.11 = (bf16[2,512,128]{2,1,0:T(8,128)(2,1)S(1)}, bf16[2,512,128]{2,1,0:T(8,128)(2,1)}, u32[]{:S(2)}, u32[]{:S(2)}) collective-permute-start(bf16[2,512,128]{2,1,0:T(8,128)(2,1)S(1)} %get-tuple-element.242), channel_id=1, source_target_pairs={{1,0},{2,1},{3,2},{4,3},{5,4},{6,5},{7,6},{9,8},{10,9},{11,10},{12... | collective-permute-start | bytes 786440 | tf_op jit(solution)/shard_map/ppermute | solution.py:18
  57.7 1.6 copy.63
  59.2 6.0 %all-to-all-start = ((bf16[32,2,32,256]{3,2,1,0:T(8,128)(2,1)}), bf16[32,2,32,256]{3,2,1,0:T(8,128)(2,1)S(1)}, u32[]{:S(2)}, u32[]{:S(2)}) async-start(bf16[32,2,32,256]{3,2,1,0:T(8,128)(2,1)} %copy.63), calls=%async_computation | async-start | bytes 2097152 | tf_op jit(solution)/shard_map/all_to_all | solution.py:91
  68.4 11.5 %while.22 = (s32[]{:T(128)}, bf16[2,512,512]{2,1,0:T(8,128)(2,1)S(1)}, s32[4,3]{1,0:T(4,128)}, bf16[4,2,256,256]{3,2,0,1:T(8,128)(2,1)S(1)}, s32[]{:T(128)}) while((s32[]{:T(128)}, bf16[2,512,512]{2,1,0:T(8,128)(2,1)S(1)}, s32[4,3]{1,0:T(4,128)}, bf16[4,2,256,256]{3,2,0,1:T(8,128)(2,1)S(1)}, s32[]{:T(128)}) %tuple.95), condition=%wide.while_cond.4, body=%wide.while_body.4.sunk | while | flops 2 | bytes 524413 | solution.py:95
  69.7 1.5 bitcast_dynamic-update-slice_fusion.2
  72.6 1.5 bitcast_dynamic-update-slice_fusion.2
  75.4 1.5 bitcast_dynamic-update-slice_fusion.2
  78.2 1.5 bitcast_dynamic-update-slice_fusion.2
  79.9 1.7 all-to-all-done
  89.6 1.3 convolution_add_fusion
  90.9 2.0 multiply_convert_fusion.1
  93.0 1.5 fusion.55
  102.0 1.8 fusion.28
  103.9 1.8 copy.86
  105.7 6.7 %all-to-all-start.1 = ((bf16[4,2,256,256]{3,0,1,2:T(4,128)(2,1)}), bf16[4,2,256,256]{3,0,1,2:T(4,128)(2,1)}, u32[]{:S(2)}, u32[]{:S(2)}) async-start(bf16[4,2,256,256]{3,0,1,2:T(4,128)(2,1)} %copy.86), calls=%async_computation.1 | async-start | bytes 2097152 | tf_op jit(solution)/shard_map/all_to_all | solution.py:146
  112.4 1.5 pad_maximum_fusion
  114.2 53.2 %while.21 = (s32[]{:T(128)}, f32[2,512,512]{2,1,0:T(8,128)S(1)}, s32[4,2]{0,1:T(2,128)S(1)}, f32[4,2,256,256]{3,2,0,1:T(8,128)}, s32[]{:T(128)}, /*index=5*/s32[1,1]{0,1:T(1,128)}, s32[]{:T(128)}, s32[1,1]{0,1:T(1,128)}) while((s32[]{:T(128)}, f32[2,512,512]{2,1,0:T(8,128)S(1)}, s32[4,2]{0,1:T(2,128)S(1)}, f32[4,2,256,256]{3,2,0,1:T(8,128)}, ...), condition=%wide.region_1.2_spmd, body=%wide.region_0.1_spmd.sunk | while | flops 131082 | bytes 2621661 | solution.py:145
  117.4 1.3 bitcast_add_fusion.2
  118.7 6.0 %dynamic_update_slice.12 = f32[2,512,512]{2,1,0:T(8,128)S(1)} dynamic-update-slice(f32[2,512,512]{2,1,0:T(8,128)S(1)} %get-tuple-element.333, f32[2,256,256]{2,1,0:T(8,128)S(1)} %bitcast_add_fusion.2, s32[]{:T(128)} %constant.220.clone.1..sunk, s32[]{:T(128)S(6)} %select_n.130, s32[]{:T(128)S(6)} %select_n.131) | dynamic-update-slice | bytes 1048580 | tf_op jit(solution)/shard_map/while/body/eval_jaxpr/dynamic_update_slice | solution.py:141
  129.1 8.7 %dynamic_update_slice.12 = f32[2,512,512]{2,1,0:T(8,128)S(1)} dynamic-update-slice(f32[2,512,512]{2,1,0:T(8,128)S(1)} %get-tuple-element.333, f32[2,256,256]{2,1,0:T(8,128)S(1)} %bitcast_add_fusion.2, s32[]{:T(128)} %constant.220.clone.1..sunk, s32[]{:T(128)S(6)} %select_n.130, s32[]{:T(128)S(6)} %select_n.131) | dynamic-update-slice | bytes 1048580 | tf_op jit(solution)/shard_map/while/body/eval_jaxpr/dynamic_update_slice | solution.py:141
  142.3 10.2 %dynamic_update_slice.12 = f32[2,512,512]{2,1,0:T(8,128)S(1)} dynamic-update-slice(f32[2,512,512]{2,1,0:T(8,128)S(1)} %get-tuple-element.333, f32[2,256,256]{2,1,0:T(8,128)S(1)} %bitcast_add_fusion.2, s32[]{:T(128)} %constant.220.clone.1..sunk, s32[]{:T(128)S(6)} %select_n.130, s32[]{:T(128)S(6)} %select_n.131) | dynamic-update-slice | bytes 1048580 | tf_op jit(solution)/shard_map/while/body/eval_jaxpr/dynamic_update_slice | solution.py:141
  157.0 10.4 %dynamic_update_slice.12 = f32[2,512,512]{2,1,0:T(8,128)S(1)} dynamic-update-slice(f32[2,512,512]{2,1,0:T(8,128)S(1)} %get-tuple-element.333, f32[2,256,256]{2,1,0:T(8,128)S(1)} %bitcast_add_fusion.2, s32[]{:T(128)} %constant.220.clone.1..sunk, s32[]{:T(128)S(6)} %select_n.130, s32[]{:T(128)S(6)} %select_n.131) | dynamic-update-slice | bytes 1048580 | tf_op jit(solution)/shard_map/while/body/eval_jaxpr/dynamic_update_slice | solution.py:141
  167.6 2.2 %collective-permute-start.12 = (bf16[2,128,512]{2,1,0:T(8,128)(2,1)S(1)}, bf16[2,128,512]{2,1,0:T(8,128)(2,1)S(1)}, u32[]{:S(2)}, u32[]{:S(2)}) collective-permute-start(bf16[2,128,512]{2,1,0:T(8,128)(2,1)S(1)} %get-tuple-element.237), channel_id=1, source_target_pairs={{0,8},{8,16},{16,24},{1,9},{9,17},{17,25},{2,10},{10,18},{18,26},{... | collective-permute-start | bytes 786440 | tf_op jit(solution)/shard_map/ppermute | solution.py:17
  169.8 3.6 %collective-permute-start.13 = (bf16[2,128,512]{2,1,0:T(8,128)(2,1)S(1)}, bf16[2,128,512]{2,1,0:T(8,128)(2,1)S(1)}, u32[]{:S(2)}, u32[]{:S(2)}) collective-permute-start(bf16[2,128,512]{2,1,0:T(8,128)(2,1)S(1)} %get-tuple-element.238), channel_id=1, source_target_pairs={{8,0},{16,8},{24,16},{9,1},{17,9},{25,17},{10,2},{18,10},{26,18},{... | collective-permute-start | bytes 786440 | tf_op jit(solution)/shard_map/ppermute | solution.py:18
  173.6 1.7 collective-permute-done.12
  175.3 2.0 collective-permute-done.13
  178.6 1.3 collective-permute-start.14
  179.9 4.6 %collective-permute-start.15 = (bf16[2,256,128]{2,1,0:T(8,128)(2,1)S(1)}, bf16[2,256,128]{2,1,0:T(8,128)(2,1)S(1)}, u32[]{:S(2)}, u32[]{:S(2)}) collective-permute-start(bf16[2,256,128]{2,1,0:T(8,128)(2,1)S(1)} %get-tuple-element.240), channel_id=1, source_target_pairs={{1,0},{2,1},{3,2},{4,3},{5,4},{6,5},{7,6},{9,8},{10,9},{11,10},{12... | collective-permute-start | bytes 393224 | tf_op jit(solution)/shard_map/ppermute | solution.py:18
  184.5 1.5 copy.114
  186.8 5.5 %convolution_convert_fusion = bf16[8,24,16384]{2,1,0:T(8,128)(2,1)S(1)} fusion(f32[8,4,24]{2,1,0:T(4,128)S(1)} %bitcast.190, bf16[8,4,16384]{2,1,0:T(4,128)(2,1)S(1)} %reshape.183), kind=kOutput, calls=%fused_computation.5 | convolution fusion | flops 154140672 | bytes 7343104 | tf_op jit(solution)/shard_map/dpk,dpx->dkx/dot_general | solution.py:148
  193.4 1.9 collective-permute-start.16
  197.2 5.3 %collective-permute-done.16 = bf16[12,2,32,256]{3,2,1,0:T(8,128)(2,1)S(1)} collective-permute-done((bf16[12,2,32,256]{3,2,1,0:T(8,128)(2,1)S(1)}, bf16[12,2,32,256]{3,2,1,0:T(8,128)(2,1)S(1)}, u32[]{:S(2)}, u32[]{:S(2)}) %collective-permute-start.16) | collective-permute-done | bytes 393248 | tf_op jit(solution)/shard_map/ppermute | solution.py:26
  (95 shorter events, 41.4 us)
Async XLA Ops:
  1.7 47.3 %collective-permute-start.8 = (bf16[2,128,256]{2,1,0:T(8,128)(2,1)S(1)}, bf16[2,128,256]{2,1,0:T(8,128)(2,1)S(1)}, u32[]{:S(2)}, u32[]{:S(2)}) collective-permute-start(bf16[2,128,256]{2,1,0:T(8,128)(2,1)S(1)} %get-tuple-element.243), channel_id=1, source_target_pairs={{0,8},{8,16},{16,24},{1,9},{9,17},{17,25},{2,10},{10,18},{18,26},{... | collective-permute-start | bytes 393224 | tf_op jit(solution)/shard_map/ppermute | solution.py:17
  3.7 45.4 %collective-permute-start.9 = (bf16[2,128,256]{2,1,0:T(8,128)(2,1)S(1)}, bf16[2,128,256]{2,1,0:T(8,128)(2,1)S(1)}, u32[]{:S(2)}, u32[]{:S(2)}) collective-permute-start(bf16[2,128,256]{2,1,0:T(8,128)(2,1)S(1)} %get-tuple-element.244), channel_id=1, source_target_pairs={{8,0},{16,8},{24,16},{9,1},{17,9},{25,17},{10,2},{18,10},{26,18},{... | collective-permute-start | bytes 393224 | tf_op jit(solution)/shard_map/ppermute | solution.py:18
  8.9 3.7 %collective-permute-start = (f32[4,24]{0,1:T(8,128)S(1)}, f32[4,24]{0,1:T(8,128)S(1)}, u32[]{:S(2)}, u32[]{:S(2)}) collective-permute-start(f32[4,24]{0,1:T(8,128)S(1)} %copy.59), channel_id=1, source_target_pairs={{0,1},{1,2},{2,3},{3,4},{4,5},{5,6},{6,7},{7,0},{8,9},{9,10},{10,1... | collective-permute-start | bytes 1160 | tf_op jit(solution)/shard_map/ppermute | solution.py:80
  12.6 4.3 %collective-permute-start.1 = (f32[4,24]{0,1:T(8,128)S(1)}, f32[4,24]{0,1:T(8,128)S(1)}, u32[]{:S(2)}, u32[]{:S(2)}) collective-permute-start(f32[4,24]{0,1:T(8,128)S(1)} %collective-permute-done), channel_id=1, source_target_pairs={{0,1},{1,2},{2,3},{3,4},{4,5},{5,6},{6,7},{7,0},{8,9},{9,10},{10,1... | collective-permute-start | bytes 1160 | tf_op jit(solution)/shard_map/ppermute | solution.py:80
  16.9 6.4 %collective-permute-start.2 = (f32[4,24]{0,1:T(8,128)S(1)}, f32[4,24]{0,1:T(8,128)S(1)}, u32[]{:S(2)}, u32[]{:S(2)}) collective-permute-start(f32[4,24]{0,1:T(8,128)S(1)} %collective-permute-done.1), channel_id=1, source_target_pairs={{0,1},{1,2},{2,3},{3,4},{4,5},{5,6},{6,7},{7,0},{8,9},{9,10},{10,1... | collective-permute-start | bytes 1160 | tf_op jit(solution)/shard_map/ppermute | solution.py:80
  23.3 6.9 %collective-permute-start.3 = (f32[4,24]{0,1:T(8,128)S(1)}, f32[4,24]{0,1:T(8,128)S(1)}, u32[]{:S(2)}, u32[]{:S(2)}) collective-permute-start(f32[4,24]{0,1:T(8,128)S(1)} %collective-permute-done.2), channel_id=1, source_target_pairs={{0,1},{1,2},{2,3},{3,4},{4,5},{5,6},{6,7},{7,0},{8,9},{9,10},{10,1... | collective-permute-start | bytes 1160 | tf_op jit(solution)/shard_map/ppermute | solution.py:80
  28.3 27.5 %collective-permute-start.7 = (bf16[1,12,2,32,256]{4,3,2,1,0:T(8,128)(2,1)}, bf16[1,12,2,32,256]{4,3,2,1,0:T(8,128)(2,1)S(1)}, u32[]{:S(2)}, u32[]{:S(2)}) collective-permute-start(bf16[1,12,2,32,256]{4,3,2,1,0:T(8,128)(2,1)} %param.18), channel_id=1, source_target_pairs={{8,0},{16,8},{24,16},{9,1},{17,9},{25,17},{10,2},{18,10},{26,18},{... | collective-permute-start | bytes 1179656 | tf_op jit(solution)/shard_map/ppermute | solution.py:26
  30.2 5.9 %collective-permute-start.4 = (f32[4,24]{0,1:T(8,128)S(1)}, f32[4,24]{0,1:T(8,128)S(1)}, u32[]{:S(2)}, u32[]{:S(2)}) collective-permute-start(f32[4,24]{0,1:T(8,128)S(1)} %collective-permute-done.3), channel_id=1, source_target_pairs={{0,1},{1,2},{2,3},{3,4},{4,5},{5,6},{6,7},{7,0},{8,9},{9,10},{10,1... | collective-permute-start | bytes 1160 | tf_op jit(solution)/shard_map/ppermute | solution.py:80
  36.1 6.4 %collective-permute-start.5 = (f32[4,24]{0,1:T(8,128)S(1)}, f32[4,24]{0,1:T(8,128)S(1)}, u32[]{:S(2)}, u32[]{:S(2)}) collective-permute-start(f32[4,24]{0,1:T(8,128)S(1)} %collective-permute-done.4), channel_id=1, source_target_pairs={{0,1},{1,2},{2,3},{3,4},{4,5},{5,6},{6,7},{7,0},{8,9},{9,10},{10,1... | collective-permute-start | bytes 1160 | tf_op jit(solution)/shard_map/ppermute | solution.py:80
  42.5 6.4 %collective-permute-start.6 = (f32[4,24]{0,1:T(8,128)S(1)}, f32[4,24]{0,1:T(8,128)S(1)}, u32[]{:S(2)}, u32[]{:S(2)}) collective-permute-start(f32[4,24]{0,1:T(8,128)S(1)} %collective-permute-done.5), channel_id=1, source_target_pairs={{0,1},{1,2},{2,3},{3,4},{4,5},{5,6},{6,7},{7,0},{8,9},{9,10},{10,1... | collective-permute-start | bytes 1160 | tf_op jit(solution)/shard_map/ppermute | solution.py:80
  49.1 6.7 %copy-start.2 = (bf16[2,128,256]{2,1,0:T(8,128)(2,1)}, bf16[2,128,256]{2,1,0:T(8,128)(2,1)S(1)}, u32[]{:S(2)}) copy-start(bf16[2,128,256]{2,1,0:T(8,128)(2,1)S(1)} %collective-permute-done.9) | copy-start | bytes 393220
  49.2 18.0 %collective-permute-start.10 = (bf16[2,512,128]{2,1,0:T(8,128)(2,1)S(1)}, bf16[2,512,128]{2,1,0:T(8,128)(2,1)}, u32[]{:S(2)}, u32[]{:S(2)}) collective-permute-start(bf16[2,512,128]{2,1,0:T(8,128)(2,1)S(1)} %get-tuple-element.241), channel_id=1, source_target_pairs={{0,1},{1,2},{2,3},{3,4},{4,5},{5,6},{6,7},{8,9},{9,10},{10,11},{11... | collective-permute-start | bytes 786440 | tf_op jit(solution)/shard_map/ppermute | solution.py:17
  50.5 16.7 %collective-permute-start.11 = (bf16[2,512,128]{2,1,0:T(8,128)(2,1)S(1)}, bf16[2,512,128]{2,1,0:T(8,128)(2,1)}, u32[]{:S(2)}, u32[]{:S(2)}) collective-permute-start(bf16[2,512,128]{2,1,0:T(8,128)(2,1)S(1)} %get-tuple-element.242), channel_id=1, source_target_pairs={{1,0},{2,1},{3,2},{4,3},{5,4},{6,5},{7,6},{9,8},{10,9},{11,10},{12... | collective-permute-start | bytes 786440 | tf_op jit(solution)/shard_map/ppermute | solution.py:18
  57.7 7.6 %copy-start.3 = (s32[1,1,4,2]{2,3,1,0:T(2,128)S(1)}, s32[1,1,4,2]{2,3,1,0:T(2,128)}, u32[]{:S(2)}) copy-start(s32[1,1,4,2]{2,3,1,0:T(2,128)} %param.20) | copy-start | bytes 100
  59.2 22.3 %all-to-all-start = ((bf16[32,2,32,256]{3,2,1,0:T(8,128)(2,1)}), bf16[32,2,32,256]{3,2,1,0:T(8,128)(2,1)S(1)}, u32[]{:S(2)}, u32[]{:S(2)}) async-start(bf16[32,2,32,256]{3,2,1,0:T(8,128)(2,1)} %copy.63), calls=%async_computation | async-start | bytes 2097152 | tf_op jit(solution)/shard_map/all_to_all | solution.py:91
  88.3 2.6 %copy-start.4 = (bf16[1,1,4,256,256]{4,3,2,1,0:T(8,128)(2,1)S(1)}, bf16[1,1,4,256,256]{4,3,2,1,0:T(8,128)(2,1)}, u32[]{:S(2)}) copy-start(bf16[1,1,4,256,256]{4,3,2,1,0:T(8,128)(2,1)} %param.23) | copy-start | bytes 1572868
  88.4 2.6 %copy-start.5 = (f32[4]{0:T(128)S(1)}, f32[4]{0:T(128)}, u32[]{:S(2)}) copy-start(f32[4]{0:T(128)} %compare_convert_fusion) | copy-start | bytes 52
  105.7 78.8 %all-to-all-start.1 = ((bf16[4,2,256,256]{3,0,1,2:T(4,128)(2,1)}), bf16[4,2,256,256]{3,0,1,2:T(4,128)(2,1)}, u32[]{:S(2)}, u32[]{:S(2)}) async-start(bf16[4,2,256,256]{3,0,1,2:T(4,128)(2,1)} %copy.86), calls=%async_computation.1 | async-start | bytes 2097152 | tf_op jit(solution)/shard_map/all_to_all | solution.py:146
  167.6 7.7 %collective-permute-start.12 = (bf16[2,128,512]{2,1,0:T(8,128)(2,1)S(1)}, bf16[2,128,512]{2,1,0:T(8,128)(2,1)S(1)}, u32[]{:S(2)}, u32[]{:S(2)}) collective-permute-start(bf16[2,128,512]{2,1,0:T(8,128)(2,1)S(1)} %get-tuple-element.237), channel_id=1, source_target_pairs={{0,8},{8,16},{16,24},{1,9},{9,17},{17,25},{2,10},{10,18},{18,26},{... | collective-permute-start | bytes 786440 | tf_op jit(solution)/shard_map/ppermute | solution.py:17
  169.8 7.5 %collective-permute-start.13 = (bf16[2,128,512]{2,1,0:T(8,128)(2,1)S(1)}, bf16[2,128,512]{2,1,0:T(8,128)(2,1)S(1)}, u32[]{:S(2)}, u32[]{:S(2)}) collective-permute-start(bf16[2,128,512]{2,1,0:T(8,128)(2,1)S(1)} %get-tuple-element.238), channel_id=1, source_target_pairs={{8,0},{16,8},{24,16},{9,1},{17,9},{25,17},{10,2},{18,10},{26,18},{... | collective-permute-start | bytes 786440 | tf_op jit(solution)/shard_map/ppermute | solution.py:18
  177.5 1.0 copy-start
  178.6 16.7 %collective-permute-start.14 = (bf16[2,256,128]{2,1,0:T(8,128)(2,1)S(1)}, bf16[2,256,128]{2,1,0:T(8,128)(2,1)S(1)}, u32[]{:S(2)}, u32[]{:S(2)}) collective-permute-start(bf16[2,256,128]{2,1,0:T(8,128)(2,1)S(1)} %get-tuple-element.239), channel_id=1, source_target_pairs={{0,1},{1,2},{2,3},{3,4},{4,5},{5,6},{6,7},{8,9},{9,10},{10,11},{11... | collective-permute-start | bytes 393224 | tf_op jit(solution)/shard_map/ppermute | solution.py:17
  179.9 15.4 %collective-permute-start.15 = (bf16[2,256,128]{2,1,0:T(8,128)(2,1)S(1)}, bf16[2,256,128]{2,1,0:T(8,128)(2,1)S(1)}, u32[]{:S(2)}, u32[]{:S(2)}) collective-permute-start(bf16[2,256,128]{2,1,0:T(8,128)(2,1)S(1)} %get-tuple-element.240), channel_id=1, source_target_pairs={{1,0},{2,1},{3,2},{4,3},{5,4},{6,5},{7,6},{9,8},{10,9},{11,10},{12... | collective-permute-start | bytes 393224 | tf_op jit(solution)/shard_map/ppermute | solution.py:18
  193.4 9.1 %collective-permute-start.16 = (bf16[12,2,32,256]{3,2,1,0:T(8,128)(2,1)S(1)}, bf16[12,2,32,256]{3,2,1,0:T(8,128)(2,1)S(1)}, u32[]{:S(2)}, u32[]{:S(2)}) collective-permute-start(bf16[12,2,32,256]{3,2,1,0:T(8,128)(2,1)S(1)} %bitcast.189), channel_id=1, source_target_pairs={{0,8},{8,16},{16,24},{1,9},{9,17},{17,25},{2,10},{10,18},{18,26},{... | collective-permute-start | bytes 1179656 | tf_op jit(solution)/shard_map/ppermute | solution.py:26
  196.3 0.8 copy-start.1
